TPU v7x, 32 devices: a whole 2x2x4 slice. The times are simulated.
32 devices in a mesh: dp: 8 (over z, y), tensor: 4 (over x, core).
Axes of the slice: x: 2, y: 2, z: 4, core: 2. Of those that a mesh axis runs over, the one named last changes fastest.
Arguments:
- layer_input: bfloat16 [16, 1024, 768], P('dp', 'tensor'), may hold values from -6 to 6
- cotangent: bfloat16 [16, 1024, 768], P('dp', 'tensor'), may hold values from -6 to 6
- segment_ids: int32 [16, 1024], P('dp'), may hold values from 0 to 15, never falling along the last dimension, each value on 1 to 512 neighbouring positions
- query_weight: bfloat16 [768, 768], P('dp', 'tensor'), may hold values from -0.21875 to 0.21875
- key_weight: bfloat16 [768, 768], P('dp', 'tensor'), may hold values from -0.21875 to 0.21875
- value_weight: bfloat16 [768, 768], P('dp', 'tensor'), may hold values from -0.21875 to 0.21875
- output_weight: bfloat16 [768, 768], P('tensor', 'dp'), may hold values from -0.875 to 0.875
- gate_weight: bfloat16 [768, 3072], P('dp', 'tensor'), may hold values from -0.21875 to 0.21875
- up_weight: bfloat16 [768, 3072], P('dp', 'tensor'), may hold values from -0.21875 to 0.21875
- down_weight: bfloat16 [3072, 768], P('tensor', 'dp'), may hold values from -0.109375 to 0.109375
- first_gain: float32 [768], replicated, may hold values from 0.5 to 1.5
- first_bias: float32 [768], replicated, may hold values from -1 to 1
- second_gain: float32 [768], replicated, may hold values from 0.5 to 1.5
- second_bias: float32 [768], replicated, may hold values from -1 to 1
Outputs:
- output: bfloat16 [16, 1024, 768], P('dp', 'tensor')
- grad_input: bfloat16 [16, 1024, 768], P('dp', 'tensor')
- grad_query_weight: float32 [768, 768], P('dp', 'tensor')
- grad_key_weight: float32 [768, 768], P('dp', 'tensor')
- grad_value_weight: float32 [768, 768], P('dp', 'tensor')
- grad_output_weight: float32 [768, 768], P('tensor', 'dp')
- grad_gate_weight: float32 [768, 3072], P('dp', 'tensor')
- grad_up_weight: float32 [768, 3072], P('dp', 'tensor')
- grad_down_weight: float32 [3072, 768], P('tensor', 'dp')
- grad_first_gain: float32 [768], replicated
- grad_first_bias: float32 [768], replicated
- grad_second_gain: float32 [768], replicated
- grad_second_bias: float32 [768], replicated
Inputs may be any that keep to these rules, and one draw needn't show every extreme that they name: `segment_ids`: ids never fall along a packed row and attention only joins tokens of equal id within one row; a document has 1 to 512 tokens, and some document has exactly that many.
All inputs are finite; a program needn't handle non-finite values.
Results may differ from a plain program's by a relative error of at most 0.023.
Values may be sent and summed in bfloat16 or wider, within the bound.
A program may use at most 128 MiB of HBM per device.

v0:
```python
import jax
import jax.numpy as jnp
from jax import lax
from jax.sharding import PartitionSpec as P

HD = 64
eps_norm = 1e-06
rope_base = 1000.0
mask_fill = -1e30


def layer_norm(field_rows, gain_vec, bias_vec):
    row_mean = jnp.mean(field_rows, axis=-1, keepdims=True)
    centred = field_rows - row_mean
    variance = jnp.mean(centred * centred, axis=-1, keepdims=True)
    return centred * lax.rsqrt(variance + eps_norm) * gain_vec + bias_vec


def rotary_tables(length, head_dim):
    half_dim = head_dim // 2
    frequency = rope_base ** (-(2.0 * jnp.arange(half_dim, dtype=jnp.float32)) / head_dim)
    angles = jnp.arange(length, dtype=jnp.float32)[:, None] * frequency[None, :]
    return (jnp.cos(angles), jnp.sin(angles))


def rotate(heads_data, cos_table, sine_table):
    half_dim = heads_data.shape[-1] // 2
    first_half = heads_data[..., :half_dim]
    second_half = heads_data[..., half_dim:]
    cos_part = cos_table[:, None, :]
    sine_part = sine_table[:, None, :]
    return jnp.concatenate(
        [
            first_half * cos_part - second_half * sine_part,
            second_half * cos_part + first_half * sine_part,
        ],
        axis=-1,
    )


def swiglu(gate_pre, up_pre):
    return jax.nn.silu(gate_pre) * up_pre


def contract_rows(left, right):
    return lax.dot_general(
        left, right, (((0,), (0,)), ((), ())), preferred_element_type=jnp.float32
    )


def times_transpose(left, right):
    return lax.dot_general(
        left, right, (((1,), (1,)), ((), ())), preferred_element_type=jnp.float32
    )


def per_device(
    layer_input,
    cotangent,
    segment_ids,
    query_weight,
    key_weight,
    value_weight,
    output_weight,
    gate_weight,
    up_weight,
    down_weight,
    first_gain,
    first_bias,
    second_gain,
    second_bias,
):
    model_width = layer_input.shape[2]
    length = segment_ids.shape[1]
    block_rows = min(512, length)
    block_count = length // block_rows
    local_heads = query_weight.shape[1] // HD
    local_width = local_heads * HD
    score_scale = HD ** (-0.5)
    cos_table, sine_table = rotary_tables(length, HD)

    def fetch_weights():
        row_parts = (
            lax.all_gather(query_weight, "dp", axis=0, tiled=True),
            lax.all_gather(key_weight, "dp", axis=0, tiled=True),
            lax.all_gather(value_weight, "dp", axis=0, tiled=True),
            lax.all_gather(gate_weight, "dp", axis=0, tiled=True),
            lax.all_gather(up_weight, "dp", axis=0, tiled=True),
        )
        col_parts = (
            lax.all_gather(output_weight, "dp", axis=1, tiled=True),
            lax.all_gather(down_weight, "dp", axis=1, tiled=True),
        )
        return tuple(row_parts) + tuple(col_parts)

    def micro_step(weights, row_input, row_cotangent, segment_row):
        query_full, key_full, value_full, gate_full, up_full, output_full, down_full = weights
        full_input = lax.all_gather(row_input, "tensor", axis=0, tiled=True)
        query_pre = jnp.dot(full_input, query_full, preferred_element_type=jnp.float32).reshape(
            length, local_heads, HD
        )
        key_pre = jnp.dot(full_input, key_full, preferred_element_type=jnp.float32).reshape(
            length, local_heads, HD
        )
        value_rows = (
            jnp.dot(full_input, value_full, preferred_element_type=jnp.float32)
            .astype(jnp.bfloat16)
            .reshape(length, local_heads, HD)
        )
        query_rows = rotate(query_pre, cos_table, sine_table).astype(jnp.bfloat16)
        key_rows = rotate(key_pre, cos_table, sine_table).astype(jnp.bfloat16)
        query_blocks = query_rows.reshape(block_count, block_rows, local_heads, HD)
        segment_blocks = segment_row.reshape(block_count, block_rows)

        def block_scores(query_block, segment_block):
            scores = (
                jnp.einsum(
                    "qhd,khd->hqk", query_block, key_rows, preferred_element_type=jnp.float32
                )
                * score_scale
            )
            allowed = segment_block[:, None] == segment_row[None, :]
            return jnp.where(allowed[None, :, :], scores, mask_fill)

        def attend_forward(block_inputs):
            scores = block_scores(block_inputs[0], block_inputs[1])
            row_max = jnp.max(scores, axis=-1, keepdims=True)
            exponent_terms = jnp.exp(scores - row_max)
            row_total = jnp.sum(exponent_terms, axis=-1, keepdims=True)
            probabilities = (exponent_terms / row_total).astype(jnp.bfloat16)
            mixed_rows = jnp.einsum(
                "hqk,khd->qhd", probabilities, value_rows, preferred_element_type=jnp.float32
            )
            return (mixed_rows, (row_max + jnp.log(row_total))[..., 0])

        mixed_blocks, log_totals = lax.map(attend_forward, (query_blocks, segment_blocks))
        attended = mixed_blocks.reshape(length, local_width).astype(jnp.bfloat16)
        attention_branch = lax.psum_scatter(
            jnp.dot(attended, output_full, preferred_element_type=jnp.float32).astype(jnp.bfloat16),
            "tensor",
            scatter_dimension=0,
            tiled=True,
        ).astype(jnp.float32)
        first_sum = row_input.astype(jnp.float32) + attention_branch
        hidden_state, first_back = jax.vjp(layer_norm, first_sum, first_gain, first_bias)
        full_hidden = lax.all_gather(
            hidden_state.astype(jnp.bfloat16), "tensor", axis=0, tiled=True
        )
        gate_pre = jnp.dot(full_hidden, gate_full, preferred_element_type=jnp.float32)
        up_pre = jnp.dot(full_hidden, up_full, preferred_element_type=jnp.float32)
        activated_exact, swiglu_back = jax.vjp(swiglu, gate_pre, up_pre)
        activated = activated_exact.astype(jnp.bfloat16)
        feed_branch = lax.psum_scatter(
            jnp.dot(activated, down_full, preferred_element_type=jnp.float32).astype(jnp.bfloat16),
            "tensor",
            scatter_dimension=0,
            tiled=True,
        ).astype(jnp.float32)
        layer_output, second_back = jax.vjp(
            layer_norm, hidden_state + feed_branch, second_gain, second_bias
        )
        grad_second_sum, grad_second_gain, grad_second_bias = second_back(
            row_cotangent.astype(jnp.float32)
        )
        grad_second_full = lax.all_gather(
            grad_second_sum.astype(jnp.bfloat16), "tensor", axis=0, tiled=True
        )
        grad_activated = times_transpose(grad_second_full, down_full)
        grad_down = contract_rows(activated, grad_second_full)
        grad_gate_pre, grad_up_pre = swiglu_back(grad_activated)
        gate_low = grad_gate_pre.astype(jnp.bfloat16)
        up_low = grad_up_pre.astype(jnp.bfloat16)
        grad_hidden = grad_second_sum + lax.psum_scatter(
            (times_transpose(gate_low, gate_full) + times_transpose(up_low, up_full)).astype(
                jnp.bfloat16
            ),
            "tensor",
            scatter_dimension=0,
            tiled=True,
        ).astype(jnp.float32)
        grad_gate = contract_rows(full_hidden, gate_low)
        grad_up = contract_rows(full_hidden, up_low)
        grad_first_sum, grad_first_gain, grad_first_bias = first_back(grad_hidden)
        grad_first_full = lax.all_gather(
            grad_first_sum.astype(jnp.bfloat16), "tensor", axis=0, tiled=True
        )
        grad_attended = (
            times_transpose(grad_first_full, output_full)
            .astype(jnp.bfloat16)
            .reshape(block_count, block_rows, local_heads, HD)
        )
        grad_output = contract_rows(attended, grad_first_full)

        def attend_backward(sums_carry, block_inputs):
            key_sum, value_sum = sums_carry
            query_block, segment_block, log_block, grad_block = block_inputs
            scores = block_scores(query_block, segment_block)
            probabilities = jnp.exp(scores - log_block[..., None])
            grad_softmax = jnp.einsum(
                "qhd,khd->hqk", grad_block, value_rows, preferred_element_type=jnp.float32
            )
            value_sum = value_sum + jnp.einsum(
                "hqk,qhd->khd",
                probabilities.astype(jnp.bfloat16),
                grad_block,
                preferred_element_type=jnp.float32,
            )
            row_inner = jnp.sum(probabilities * grad_softmax, axis=-1, keepdims=True)
            grad_scores = (probabilities * (grad_softmax - row_inner)).astype(jnp.bfloat16)
            grad_query_block = (
                jnp.einsum(
                    "hqk,khd->qhd", grad_scores, key_rows, preferred_element_type=jnp.float32
                )
                * score_scale
            )
            key_sum = (
                key_sum
                + jnp.einsum(
                    "hqk,qhd->khd", grad_scores, query_block, preferred_element_type=jnp.float32
                )
                * score_scale
            )
            return ((key_sum, value_sum), grad_query_block)

        zero_heads = jnp.zeros((length, local_heads, HD), jnp.float32)
        (grad_key_rot, grad_value_rows), grad_query_blocks = lax.scan(
            attend_backward,
            (zero_heads, zero_heads),
            (query_blocks, segment_blocks, log_totals, grad_attended),
        )
        grad_query_low = (
            rotate(grad_query_blocks.reshape(length, local_heads, HD), cos_table, -sine_table)
            .astype(jnp.bfloat16)
            .reshape(length, local_width)
        )
        grad_key_low = (
            rotate(grad_key_rot, cos_table, -sine_table)
            .astype(jnp.bfloat16)
            .reshape(length, local_width)
        )
        grad_value_low = grad_value_rows.astype(jnp.bfloat16).reshape(length, local_width)
        query_part = times_transpose(grad_query_low, query_full)
        key_part = times_transpose(grad_key_low, key_full)
        value_part = times_transpose(grad_value_low, value_full)
        grad_input = grad_first_sum + lax.psum_scatter(
            (query_part + key_part + value_part).astype(jnp.bfloat16),
            "tensor",
            scatter_dimension=0,
            tiled=True,
        ).astype(jnp.float32)
        row_grads = (
            contract_rows(full_input, grad_query_low),
            contract_rows(full_input, grad_key_low),
            contract_rows(full_input, grad_value_low),
            grad_gate,
            grad_up,
        )
        col_grads = (grad_output, grad_down)
        norm_parts = (grad_first_gain, grad_first_bias, grad_second_gain, grad_second_bias)
        return (
            layer_output.astype(jnp.bfloat16),
            grad_input.astype(jnp.bfloat16),
            (row_grads, col_grads, norm_parts),
        )

    norm_zero = tuple(
        (
            jnp.zeros(gain_like.shape, jnp.float32)
            for gain_like in (first_gain, first_bias, second_gain, second_bias)
        )
    )
    row_zero = tuple(
        (
            jnp.zeros((model_width, weight_part.shape[1]), jnp.float32)
            for weight_part in (query_weight, key_weight, value_weight, gate_weight, up_weight)
        )
    )
    col_zero = (
        jnp.zeros((output_weight.shape[0], model_width), jnp.float32),
        jnp.zeros((down_weight.shape[0], model_width), jnp.float32),
    )

    def scan_step(totals, batch_rows):
        weights = fetch_weights()
        layer_output, grad_input, grad_terms = micro_step(
            weights, batch_rows[0], batch_rows[1], batch_rows[2]
        )
        return (jax.tree.map(jnp.add, totals, grad_terms), (layer_output, grad_input))

    totals, (outputs, grad_inputs) = lax.scan(
        scan_step, (row_zero, col_zero, norm_zero), (layer_input, cotangent, segment_ids)
    )
    row_grads, col_grads, norm_parts = totals
    row_done = lax.psum_scatter(row_grads, "dp", scatter_dimension=0, tiled=True)
    col_done = (
        lax.psum_scatter(col_grads[0], "dp", scatter_dimension=1, tiled=True),
        lax.psum_scatter(col_grads[1], "dp", scatter_dimension=1, tiled=True),
    )
    norm_done = lax.psum(norm_parts, ("dp", "tensor"))
    totals = (tuple(row_done), tuple(col_done), tuple(norm_done))
    row_done, col_done, norm_done = totals
    return (
        outputs,
        grad_inputs,
        row_done[0],
        row_done[1],
        row_done[2],
        col_done[0],
        row_done[3],
        row_done[4],
        col_done[1],
        norm_done[0],
        norm_done[1],
        norm_done[2],
        norm_done[3],
    )


def solution(mesh):
    in_specs = (
        P("dp", "tensor", None),
        P("dp", "tensor", None),
        P("dp", None),
        P("dp", "tensor"),
        P("dp", "tensor"),
        P("dp", "tensor"),
        P("tensor", "dp"),
        P("dp", "tensor"),
        P("dp", "tensor"),
        P("tensor", "dp"),
        P(),
        P(),
        P(),
        P(),
    )
    out_specs = (
        P("dp", "tensor", None),
        P("dp", "tensor", None),
        P("dp", "tensor"),
        P("dp", "tensor"),
        P("dp", "tensor"),
        P("tensor", "dp"),
        P("dp", "tensor"),
        P("dp", "tensor"),
        P("tensor", "dp"),
        P(),
        P(),
        P(),
        P(),
    )
    return jax.shard_map(
        per_device, mesh=mesh, in_specs=in_specs, out_specs=out_specs, check_vma=False
    )
```

profile of v0, /device:TPU:0, one launch (start us, length us, event | category | flops | bytes accessed | tf_op | source)
XLA Modules:
  0.0 1512.0 jit_solution(8653085761068801146)
XLA Ops:
  9.7 1014.8 %while.85 = (s32[]{:T(128)}, f32[768,192]{0,1:T(8,128)}, f32[768,192]{0,1:T(8,128)}, f32[768,192]{0,1:T(8,128)}, f32[768,768]{1,0:T(8,128)}, /*index=5*/f32[768,...) while((s32[]{:T(128)}, f32[768,192]{0,1:T(8,128)}, ...), condition=%wide.region_24.25_spmd.clone.clone.clone.clone, body=%wide.region_0.24_spmd.clone.clone.clone.clone.sunk | while | flops 15999043584 | bytes 421072320 | solution.py:290
  13.5 33.2 %all_gather.98 = bf16[192,768]{0,1:T(8,128)(2,1)S(1)} all-gather(bf16[192,96]{0,1:T(8,128)(2,1)} %get-tuple-element.1606), channel_id=1, replica_groups=mesh['dp'=8,'tensor'=4] {'dp'}, dimensions={1}, use_global_device_ids=true | all-gather | bytes 331776 | tf_op jit(solution)/shard_map/while/body/eval_jaxpr/all_gather | solution.py:91
  46.6 31.4 %all_gather.97 = bf16[768,192]{1,0:T(8,128)(2,1)S(1)} all-gather(bf16[96,192]{1,0:T(8,128)(2,1)} %get-tuple-element.1603), channel_id=1, replica_groups=mesh['dp'=8,'tensor'=4] {'dp'}, dimensions={0}, use_global_device_ids=true | all-gather | bytes 331776 | tf_op jit(solution)/shard_map/while/body/eval_jaxpr/all_gather | solution.py:86
  78.1 31.3 %all_gather.95 = bf16[768,192]{1,0:T(8,128)(2,1)S(1)} all-gather(bf16[96,192]{1,0:T(8,128)(2,1)} %get-tuple-element.1602), channel_id=1, replica_groups=mesh['dp'=8,'tensor'=4] {'dp'}, dimensions={0}, use_global_device_ids=true | all-gather | bytes 331776 | tf_op jit(solution)/shard_map/while/body/eval_jaxpr/all_gather | solution.py:85
  109.4 31.0 %all_gather.96 = bf16[768,192]{1,0:T(8,128)(2,1)S(1)} all-gather(bf16[96,192]{1,0:T(8,128)(2,1)S(1)} %copy-done.33), channel_id=1, replica_groups=mesh['dp'=8,'tensor'=4] {'dp'}, dimensions={0}, use_global_device_ids=true | all-gather | bytes 331776 | tf_op jit(solution)/shard_map/while/body/eval_jaxpr/all_gather | solution.py:84
  161.5 28.5 %reduce-scatter.28.cloned.1.call-done = bf16[256,768]{1,0:T(8,128)(2,1)} async-done(((bf16[1024,768]{1,0:T(8,128)(2,1)}), bf16[256,768]{1,0:T(8,128)(2,1)}) %reduce-scatter.28.cloned.1.call-update) | async-done | bytes 393232 | tf_op jit(solution)/shard_map/while/body/eval_jaxpr/reduce_scatter | solution.py:138
  230.2 39.1 %all-gather.20.cloned.1.call-done = bf16[768,768]{1,0:T(8,128)(2,1)} async-done(((bf16[96,768]{1,0:T(8,128)(2,1)}), bf16[768,768]{1,0:T(8,128)(2,1)}) %all-gather.20.cloned.1.call-update) | async-done | bytes 1179664 | tf_op jit(solution)/shard_map/while/body/eval_jaxpr/all_gather | solution.py:88
  275.7 36.1 %all-gather.22.cloned.1.call-done = bf16[768,768]{0,1:T(8,128)(2,1)} async-done(((bf16[768,96]{0,1:T(8,128)(2,1)}), bf16[768,768]{0,1:T(8,128)(2,1)}) %all-gather.22.cloned.1.call-update) | async-done | bytes 1179664 | tf_op jit(solution)/shard_map/while/body/eval_jaxpr/all_gather | solution.py:92
  438.1 40.8 %while.87 = (s32[]{:T(128)}, f32[1024,3,64]{0,2,1:T(8,128)S(1)}, f32[1024,3,64]{0,2,1:T(8,128)}, f32[2,512,3,64]{1,0,3,2:T(2,128)}, bf16[2,512,3,64]{1,3,2,0:T(8...) while((s32[]{:T(128)}, f32[1024,3,64]{0,2,1:T(8,128)S(1)}, ...), condition=%wide.region_18.18_spmd.clone, body=%wide.region_16.17_spmd.clone.sunk | while | flops 1031830016 | bytes 56418472 | solution.py:226
  521.0 31.5 %all_gather.98 = bf16[192,768]{0,1:T(8,128)(2,1)S(1)} all-gather(bf16[192,96]{0,1:T(8,128)(2,1)} %get-tuple-element.1606), channel_id=1, replica_groups=mesh['dp'=8,'tensor'=4] {'dp'}, dimensions={1}, use_global_device_ids=true | all-gather | bytes 331776 | tf_op jit(solution)/shard_map/while/body/eval_jaxpr/all_gather | solution.py:91
  552.5 31.4 %all_gather.97 = bf16[768,192]{1,0:T(8,128)(2,1)S(1)} all-gather(bf16[96,192]{1,0:T(8,128)(2,1)} %get-tuple-element.1603), channel_id=1, replica_groups=mesh['dp'=8,'tensor'=4] {'dp'}, dimensions={0}, use_global_device_ids=true | all-gather | bytes 331776 | tf_op jit(solution)/shard_map/while/body/eval_jaxpr/all_gather | solution.py:86
  583.9 31.4 %all_gather.95 = bf16[768,192]{1,0:T(8,128)(2,1)S(1)} all-gather(bf16[96,192]{1,0:T(8,128)(2,1)} %get-tuple-element.1602), channel_id=1, replica_groups=mesh['dp'=8,'tensor'=4] {'dp'}, dimensions={0}, use_global_device_ids=true | all-gather | bytes 331776 | tf_op jit(solution)/shard_map/while/body/eval_jaxpr/all_gather | solution.py:85
  615.3 31.0 %all_gather.96 = bf16[768,192]{1,0:T(8,128)(2,1)S(1)} all-gather(bf16[96,192]{1,0:T(8,128)(2,1)S(1)} %copy-done.33), channel_id=1, replica_groups=mesh['dp'=8,'tensor'=4] {'dp'}, dimensions={0}, use_global_device_ids=true | all-gather | bytes 331776 | tf_op jit(solution)/shard_map/while/body/eval_jaxpr/all_gather | solution.py:84
  735.1 39.1 %all-gather.20.cloned.1.call-done = bf16[768,768]{1,0:T(8,128)(2,1)} async-done(((bf16[96,768]{1,0:T(8,128)(2,1)}), bf16[768,768]{1,0:T(8,128)(2,1)}) %all-gather.20.cloned.1.call-update) | async-done | bytes 1179664 | tf_op jit(solution)/shard_map/while/body/eval_jaxpr/all_gather | solution.py:88
  780.6 36.1 %all-gather.22.cloned.1.call-done = bf16[768,768]{0,1:T(8,128)(2,1)} async-done(((bf16[768,96]{0,1:T(8,128)(2,1)}), bf16[768,768]{0,1:T(8,128)(2,1)}) %all-gather.22.cloned.1.call-update) | async-done | bytes 1179664 | tf_op jit(solution)/shard_map/while/body/eval_jaxpr/all_gather | solution.py:92
  884.7 28.3 %reduce-scatter.32.cloned.1.call-done = bf16[256,768]{1,0:T(8,128)(2,1)} async-done(((bf16[1024,768]{1,0:T(8,128)(2,1)}), bf16[256,768]{1,0:T(8,128)(2,1)}) %reduce-scatter.32.cloned.1.call-update) | async-done | bytes 393232 | tf_op jit(solution)/shard_map/while/body/eval_jaxpr/reduce_scatter | solution.py:173
  943.0 40.5 %while.87 = (s32[]{:T(128)}, f32[1024,3,64]{0,2,1:T(8,128)S(1)}, f32[1024,3,64]{0,2,1:T(8,128)}, f32[2,512,3,64]{1,0,3,2:T(2,128)}, bf16[2,512,3,64]{1,3,2,0:T(8...) while((s32[]{:T(128)}, f32[1024,3,64]{0,2,1:T(8,128)S(1)}, ...), condition=%wide.region_18.18_spmd.clone, body=%wide.region_16.17_spmd.clone.sunk | while | flops 1031830016 | bytes 56418472 | solution.py:226
  1036.1 39.7 %all-reduce = (f32[768]{0:T(1024)}, f32[768]{0:T(1024)}, f32[768]{0:T(1024)}, f32[768]{0:T(1024)}) all-reduce(f32[768]{0:T(1024)S(1)} %copy-done.58, f32[768]{0:T(1024)S(1)} %copy-done.55, f32[768]{0:T(1024)S(1)} %copy-done.52, f32[768]{0:T(1024)S(1)} %copy-done.49), channel_id=1, replica_groups=mesh['dp'=8,'tensor'=4] {'dp','tensor'}, use_global_device_ids=true, to_apply=%region_32.33 | all-reduce | flops 3072 | bytes 24576 | tf_op jit(solution)/shard_map/psum | solution.py:299
  1092.5 64.2 %reduce-scatter.14.cloned.1.call-done = f32[96,192]{1,0:T(8,128)} async-done(((f32[768,192]{1,0:T(8,128)}), f32[96,192]{1,0:T(8,128)}) %reduce-scatter.14.cloned.1.call-update) | async-done | bytes 73744 | tf_op jit(solution)/shard_map/reduce_scatter | solution.py:294
  1156.7 65.5 %reduce-scatter.16.cloned.1.call-done = f32[96,192]{1,0:T(8,128)} async-done(((f32[768,192]{1,0:T(8,128)}), f32[96,192]{1,0:T(8,128)}) %reduce-scatter.16.cloned.1.call-update) | async-done | bytes 73744 | tf_op jit(solution)/shard_map/reduce_scatter | solution.py:294
  1222.2 65.8 %reduce-scatter.18.cloned.1.call-done = f32[96,192]{1,0:T(8,128)} async-done(((f32[768,192]{1,0:T(8,128)}), f32[96,192]{1,0:T(8,128)}) %reduce-scatter.18.cloned.1.call-update) | async-done | bytes 73744 | tf_op jit(solution)/shard_map/reduce_scatter | solution.py:294
  1288.0 72.2 %reduce-scatter.20.cloned.1.call-done = f32[96,768]{1,0:T(8,128)} async-done(((f32[768,768]{1,0:T(8,128)}), f32[96,768]{1,0:T(8,128)}) %reduce-scatter.20.cloned.1.call-update) | async-done | bytes 294928 | tf_op jit(solution)/shard_map/reduce_scatter | solution.py:294
  1360.1 72.1 %reduce-scatter.22.cloned.1.call-done = f32[96,768]{1,0:T(8,128)} async-done(((f32[768,768]{1,0:T(8,128)}), f32[96,768]{1,0:T(8,128)}) %reduce-scatter.22.cloned.1.call-update) | async-done | bytes 294928 | tf_op jit(solution)/shard_map/reduce_scatter | solution.py:294
  1432.2 72.0 %reduce-scatter.24.cloned.1.call-done = f32[768,96]{0,1:T(8,128)} async-done(((f32[768,768]{0,1:T(8,128)}), f32[768,96]{0,1:T(8,128)}) %reduce-scatter.24.cloned.1.call-update) | async-done | bytes 294928 | tf_op jit(solution)/shard_map/reduce_scatter | solution.py:297
  (566 shorter events, 604.8 us)
Async XLA Ops:
  9.7 131.9 %all-gather.14.cloned.1.call-start = ((), (), s32[]{:S(2)}) async-start(), calls=%async_computation.18 | async-start | bytes 1966080 | tf_op jit(solution)/shard_map/while/body/eval_jaxpr/all_gather | solution.py:98
  11.5 178.5 %reduce-scatter.28.cloned.1.call-start = ((), (), s32[]{:S(2)}) async-start(), calls=%async_computation.19 | async-start | bytes 1966080 | tf_op jit(solution)/shard_map/while/body/eval_jaxpr/reduce_scatter | solution.py:138
  161.4 64.0 %all-gather.16.cloned.1.call-start = ((), (), s32[]{:S(2)}) async-start(), calls=%async_computation.20 | async-start | bytes 1966080 | tf_op jit(solution)/shard_map/while/body/eval_jaxpr/all_gather | solution.py:146
  194.5 74.7 %all-gather.20.cloned.1.call-start = ((), (), s32[]{:S(2)}) async-start(), calls=%async_computation.22 | async-start | bytes 1327104 | tf_op jit(solution)/shard_map/while/body/eval_jaxpr/all_gather | solution.py:88
  195.1 116.6 %all-gather.22.cloned.1.call-start = ((), (), s32[]{:S(2)}) async-start(), calls=%async_computation.23 | async-start | bytes 1327104 | tf_op jit(solution)/shard_map/while/body/eval_jaxpr/all_gather | solution.py:92
  195.9 147.1 %reduce-scatter.30.cloned.1.call-start = ((), (), s32[]{:S(2)}) async-start(), calls=%async_computation.24 | async-start | bytes 1966080 | tf_op jit(solution)/shard_map/while/body/eval_jaxpr/reduce_scatter | solution.py:153
  349.4 58.6 %reduce-scatter.32.cloned.1.call-start = ((), (), s32[]{:S(2)}) async-start(), calls=%async_computation.26 | async-start | bytes 1966080 | tf_op jit(solution)/shard_map/while/body/eval_jaxpr/reduce_scatter | solution.py:173
  379.7 54.2 %all-gather.26.cloned.1.call-start = ((), (), s32[]{:S(2)}) async-start(), calls=%async_computation.27 | async-start | bytes 1966080 | tf_op jit(solution)/shard_map/while/body/eval_jaxpr/all_gather | solution.py:184
  414.3 100.8 %reduce-scatter.34.cloned.1.call-start = ((), (), s32[]{:S(2)}) async-start(), calls=%async_computation.28 | async-start | bytes 1966080 | tf_op jit(solution)/shard_map/while/body/eval_jaxpr/reduce_scatter | solution.py:245
  517.2 130.3 %all-gather.14.cloned.1.call-start = ((), (), s32[]{:S(2)}) async-start(), calls=%async_computation.18 | async-start | bytes 1966080 | tf_op jit(solution)/shard_map/while/body/eval_jaxpr/all_gather | solution.py:98
  519.1 175.9 %reduce-scatter.28.cloned.1.call-start = ((), (), s32[]{:S(2)}) async-start(), calls=%async_computation.19 | async-start | bytes 1966080 | tf_op jit(solution)/shard_map/while/body/eval_jaxpr/reduce_scatter | solution.py:138
  667.4 62.9 %all-gather.16.cloned.1.call-start = ((), (), s32[]{:S(2)}) async-start(), calls=%async_computation.20 | async-start | bytes 1966080 | tf_op jit(solution)/shard_map/while/body/eval_jaxpr/all_gather | solution.py:146
  699.5 74.7 %all-gather.20.cloned.1.call-start = ((), (), s32[]{:S(2)}) async-start(), calls=%async_computation.22 | async-start | bytes 1327104 | tf_op jit(solution)/shard_map/while/body/eval_jaxpr/all_gather | solution.py:88
  700.1 116.6 %all-gather.22.cloned.1.call-start = ((), (), s32[]{:S(2)}) async-start(), calls=%async_computation.23 | async-start | bytes 1327104 | tf_op jit(solution)/shard_map/while/body/eval_jaxpr/all_gather | solution.py:92
  700.8 147.1 %reduce-scatter.30.cloned.1.call-start = ((), (), s32[]{:S(2)}) async-start(), calls=%async_computation.24 | async-start | bytes 1966080 | tf_op jit(solution)/shard_map/while/body/eval_jaxpr/reduce_scatter | solution.py:153
  854.4 58.6 %reduce-scatter.32.cloned.1.call-start = ((), (), s32[]{:S(2)}) async-start(), calls=%async_computation.26 | async-start | bytes 1966080 | tf_op jit(solution)/shard_map/while/body/eval_jaxpr/reduce_scatter | solution.py:173
  919.3 100.6 %reduce-scatter.34.cloned.1.call-start = ((), (), s32[]{:S(2)}) async-start(), calls=%async_computation.28 | async-start | bytes 1966080 | tf_op jit(solution)/shard_map/while/body/eval_jaxpr/reduce_scatter | solution.py:245
  1024.5 66.3 %reduce-scatter.26.cloned.1.call-start = ((), (), s32[]{:S(2)}) async-start(), calls=%async_computation.17 | async-start | bytes 884736
  1026.9 129.8 %reduce-scatter.14.cloned.1.call-start = ((), (), s32[]{:S(2)}) async-start(), calls=%async_computation.11 | async-start | bytes 884736 | tf_op jit(solution)/shard_map/reduce_scatter | solution.py:294
  1029.2 193.0 %reduce-scatter.16.cloned.1.call-start = ((), (), s32[]{:S(2)}) async-start(), calls=%async_computation.12 | async-start | bytes 884736 | tf_op jit(solution)/shard_map/reduce_scatter | solution.py:294
  1030.5 257.5 %reduce-scatter.18.cloned.1.call-start = ((), (), s32[]{:S(2)}) async-start(), calls=%async_computation.13 | async-start | bytes 884736 | tf_op jit(solution)/shard_map/reduce_scatter | solution.py:294
  1031.7 328.4 %reduce-scatter.20.cloned.1.call-start = ((), (), s32[]{:S(2)}) async-start(), calls=%async_computation.14 | async-start | bytes 2654208 | tf_op jit(solution)/shard_map/reduce_scatter | solution.py:294
  1032.5 399.7 %reduce-scatter.22.cloned.1.call-start = ((), (), s32[]{:S(2)}) async-start(), calls=%async_computation.15 | async-start | bytes 2654208 | tf_op jit(solution)/shard_map/reduce_scatter | solution.py:294
  1033.2 470.9 %reduce-scatter.24.cloned.1.call-start = ((), (), s32[]{:S(2)}) async-start(), calls=%async_computation.16 | async-start | bytes 2654208 | tf_op jit(solution)/shard_map/reduce_scatter | solution.py:297
  (136 other events, 1879.1 us)
Sparse Core Ops, SparseCore 0:
  12.1 22.3 all-gather.13
  161.0 29.0 reduce-scatter.27
  316.3 26.6 reduce-scatter.29
  379.8 28.1 reduce-scatter.31
  486.9 28.1 reduce-scatter.33
  519.3 19.6 all-gather.13
  666.9 28.0 reduce-scatter.27
  821.2 26.6 reduce-scatter.29
  884.8 28.1 reduce-scatter.31
  991.6 28.1 reduce-scatter.33
Sparse Core Ops, SparseCore 1:
  163.5 42.3 all-gather.17
  207.4 18.0 all-gather.15
  227.7 41.5 all-gather.19
  271.7 40.0 all-gather.21
  349.5 19.5 all-gather.23
  414.4 19.5 all-gather.25
  669.5 41.3 all-gather.17
  712.4 17.9 all-gather.15
  732.6 41.5 all-gather.19
  776.6 40.0 all-gather.21
  854.5 19.5 all-gather.23
  919.3 19.5 all-gather.25
  1028.3 62.5 reduce-scatter.25
  1095.1 61.5 reduce-scatter.13
  1160.6 61.5 reduce-scatter.15
  1226.4 61.5 reduce-scatter.17
  1292.1 68.0 reduce-scatter.19
  1364.2 67.9 reduce-scatter.21
  1436.1 68.0 reduce-scatter.23
where the time goes:
time: 1520 us; the launch traced here: 1510 us
  waiting for transfers between devices  898 us (59%)
  blocking collectives  292 us (19%)
  matrix products  147 us (10%)
  local copies, waits for them, and re-layouts  78.3 us (5%)
  other arithmetic  72.1 us (5%)
  between operations  16.2 us (1%)
    reduce_scatter x5, waiting for transfers between devices, per_device(): lax.psum_scatter(row_grads, 'dp', scatter_dimension=0, tiled=True)  340 us
    all_gather x2, waiting for transfers between devices, fetch_weights(): lax.all_gather(up_weight, 'dp', axis=0, tiled=True)  78.1 us
    all_gather x2, waiting for transfers between devices, fetch_weights(): lax.all_gather(down_weight, 'dp', axis=1, tiled=True)  72.2 us
    reduce_scatter x1, waiting for transfers between devices, per_device(): lax.psum_scatter(col_grads[1], 'dp', scatter_dimension=1, tiled=True)  72 us
    all_gather x2, blocking collectives, fetch_weights(): lax.all_gather(output_weight, 'dp', axis=1, tiled=True)  64.6 us
    all_gather x2, blocking collectives, fetch_weights(): lax.all_gather(value_weight, 'dp', axis=0, tiled=True)  62.8 us
    all_gather x2, blocking collectives, fetch_weights(): lax.all_gather(key_weight, 'dp', axis=0, tiled=True)  62.8 us
    all_gather x2, blocking collectives, fetch_weights(): lax.all_gather(query_weight, 'dp', axis=0, tiled=True)  61.9 us
  transfers between devices with their start and end apart: 29, of which 27 were waited for; matrix products, arithmetic and copies ran while one was open for 5% of the time, Pallas kernels for 0%

commit v1 on v0

--- a/solution.py
+++ b/solution.py
@@ -7,6 +7,28 @@
 eps_norm = 1e-06
 rope_base = 1000.0
 mask_fill = -1e30
+
+
+def in_order(blocks, dim):
+    shape = list(blocks.shape[1:])
+    shape[dim] *= blocks.shape[0]
+    return jnp.moveaxis(blocks, 0, dim).reshape(shape)
+
+
+def grow_blocks(array, axis):
+    devices = lax.axis_size(axis)
+    blocks = array[None]
+    for level in range(devices.bit_length() - 1):
+        bit = 1 << level
+        received = lax.ppermute(blocks, axis, [(i, i ^ bit) for i in range(devices)])
+        both = jnp.stack([blocks, received])
+        upper = lax.axis_index(axis) >> level & 1
+        blocks = jnp.where(upper == 0, both, both[::-1]).reshape(-1, *array.shape)
+    return blocks
+
+
+def gather_by_bits(x, axis, dim):
+    return in_order(grow_blocks(x, axis), dim)
 
 
 def layer_norm(field_rows, gain_vec, bias_vec):
@@ -82,7 +104,7 @@
     def fetch_weights():
         row_parts = (
             lax.all_gather(query_weight, "dp", axis=0, tiled=True),
-            lax.all_gather(key_weight, "dp", axis=0, tiled=True),
+            gather_by_bits(key_weight, "dp", 0),
             lax.all_gather(value_weight, "dp", axis=0, tiled=True),
             lax.all_gather(gate_weight, "dp", axis=0, tiled=True),
             lax.all_gather(up_weight, "dp", axis=0, tiled=True),

time: 1520 us -> 1460 us (0.961)
  blocking collectives: 292 us -> 228 us
    all_gather x2 -> x0, blocking collectives: 62.8 us -> none  [fetch_weights(): lax.all_gather(key_weight, 'dp', axis=0, tiled=True)]
  transfers between devices with their start and end apart: 29 -> 34, of which waited for: 27 -> 28; matrix products, arithmetic and copies ran while one was open for 5% -> 5% of each run, Pallas kernels for 0% -> 0%
where the time goes in v1:
time: 1460 us; the launch traced here: 1450 us
  waiting for transfers between devices  900 us (62%)
  blocking collectives  228 us (16%)
  matrix products  144 us (10%)
  local copies, waits for them, and re-layouts  79.1 us (5%)
  other arithmetic  70.9 us (5%)
  between operations  16.2 us (1%)
    reduce_scatter x5, waiting for transfers between devices, per_device(): lax.psum_scatter(row_grads, 'dp', scatter_dimension=0, tiled=True)  340 us
    all_gather x2, waiting for transfers between devices, fetch_weights(): lax.all_gather(up_weight, 'dp', axis=0, tiled=True)  78.2 us
    all_gather x2, waiting for transfers between devices, fetch_weights(): lax.all_gather(down_weight, 'dp', axis=1, tiled=True)  72.1 us
    reduce_scatter x1, waiting for transfers between devices, per_device(): lax.psum_scatter(col_grads[1], 'dp', scatter_dimension=1, tiled=True)  72 us
    all_gather x2, blocking collectives, fetch_weights(): lax.all_gather(value_weight, 'dp', axis=0, tiled=True)  63.2 us
    all_gather x2, blocking collectives, fetch_weights(): lax.all_gather(output_weight, 'dp', axis=1, tiled=True)  62.9 us
    all_gather x2, blocking collectives, fetch_weights(): lax.all_gather(query_weight, 'dp', axis=0, tiled=True)  62 us
    reduce_scatter x2, waiting for transfers between devices, micro_step(): lax.psum_scatter((times_transpose(gate_low, gate_full) + times_transpose(...  56.5 us
  transfers between devices with their start and end apart: 34, of which 28 were waited for; matrix products, arithmetic and copies ran while one was open for 5% of the time, Pallas kernels for 0%

profile of v1, /device:TPU:0, one launch (start us, length us, event | category | flops | bytes accessed | tf_op | source)
XLA Modules:
  0.0 1453.5 jit_solution(3627215957472515313)
XLA Ops:
  14.8 951.0 %while.95 = (s32[]{:T(128)}, f32[768,192]{0,1:T(8,128)}, f32[768,192]{0,1:T(8,128)}, f32[768,192]{0,1:T(8,128)}, f32[768,768]{1,0:T(8,128)}, /*index=5*/f32[768,...) while((s32[]{:T(128)}, f32[768,192]{0,1:T(8,128)}, ...), condition=%wide.region_24.25_spmd.clone.clone.clone.clone, body=%wide.region_0.24_spmd.clone.clone.clone.clone.sunk | while | flops 15999522816 | bytes 433993472 | solution.py:312
  19.9 31.5 %all_gather.98 = bf16[192,768]{0,1:T(8,128)(2,1)S(1)} all-gather(bf16[192,96]{0,1:T(8,128)(2,1)} %get-tuple-element.1705), channel_id=1, replica_groups=mesh['dp'=8,'tensor'=4] {'dp'}, dimensions={1}, use_global_device_ids=true | all-gather | bytes 331776 | tf_op jit(solution)/shard_map/while/body/eval_jaxpr/all_gather | solution.py:113
  52.0 31.6 %all_gather.97 = bf16[768,192]{1,0:T(8,128)(2,1)S(1)} all-gather(bf16[96,192]{1,0:T(8,128)(2,1)} %get-tuple-element.1702), channel_id=1, replica_groups=mesh['dp'=8,'tensor'=4] {'dp'}, dimensions={0}, use_global_device_ids=true | all-gather | bytes 331776 | tf_op jit(solution)/shard_map/while/body/eval_jaxpr/all_gather | solution.py:108
  85.0 31.1 %all_gather.96 = bf16[768,192]{1,0:T(8,128)(2,1)S(1)} all-gather(bf16[96,192]{1,0:T(8,128)(2,1)S(1)} %copy-done.36), channel_id=1, replica_groups=mesh['dp'=8,'tensor'=4] {'dp'}, dimensions={0}, use_global_device_ids=true | all-gather | bytes 331776 | tf_op jit(solution)/shard_map/while/body/eval_jaxpr/all_gather | solution.py:106
  135.2 27.3 %reduce-scatter.28.cloned.1.call-done = bf16[256,768]{1,0:T(8,128)(2,1)} async-done(((bf16[1024,768]{1,0:T(8,128)(2,1)}), bf16[256,768]{1,0:T(8,128)(2,1)}) %reduce-scatter.28.cloned.1.call-update) | async-done | bytes 393232 | tf_op jit(solution)/shard_map/while/body/eval_jaxpr/reduce_scatter | solution.py:160
  202.6 39.1 %all-gather.20.cloned.1.call-done = bf16[768,768]{1,0:T(8,128)(2,1)} async-done(((bf16[96,768]{1,0:T(8,128)(2,1)}), bf16[768,768]{1,0:T(8,128)(2,1)}) %all-gather.20.cloned.1.call-update) | async-done | bytes 1179664 | tf_op jit(solution)/shard_map/while/body/eval_jaxpr/all_gather | solution.py:110
  248.1 36.0 %all-gather.22.cloned.1.call-done = bf16[768,768]{0,1:T(8,128)(2,1)} async-done(((bf16[768,96]{0,1:T(8,128)(2,1)}), bf16[768,768]{0,1:T(8,128)(2,1)}) %all-gather.22.cloned.1.call-update) | async-done | bytes 1179664 | tf_op jit(solution)/shard_map/while/body/eval_jaxpr/all_gather | solution.py:114
  352.1 28.3 %reduce-scatter.32.cloned.1.call-done = bf16[256,768]{1,0:T(8,128)(2,1)} async-done(((bf16[1024,768]{1,0:T(8,128)(2,1)}), bf16[256,768]{1,0:T(8,128)(2,1)}) %reduce-scatter.32.cloned.1.call-update) | async-done | bytes 393232 | tf_op jit(solution)/shard_map/while/body/eval_jaxpr/reduce_scatter | solution.py:195
  410.5 40.8 %while.97 = (s32[]{:T(128)}, f32[1024,3,64]{0,2,1:T(8,128)S(1)}, f32[1024,3,64]{0,2,1:T(8,128)}, f32[2,512,3,64]{1,0,3,2:T(2,128)}, bf16[2,512,3,64]{1,3,2,0:T(8...) while((s32[]{:T(128)}, f32[1024,3,64]{0,2,1:T(8,128)S(1)}, ...), condition=%wide.region_18.18_spmd.clone, body=%wide.region_16.17_spmd.clone.sunk | while | flops 1031830016 | bytes 56418472 | solution.py:248
  494.3 31.3 %all_gather.98 = bf16[192,768]{0,1:T(8,128)(2,1)S(1)} all-gather(bf16[192,96]{0,1:T(8,128)(2,1)} %get-tuple-element.1705), channel_id=1, replica_groups=mesh['dp'=8,'tensor'=4] {'dp'}, dimensions={1}, use_global_device_ids=true | all-gather | bytes 331776 | tf_op jit(solution)/shard_map/while/body/eval_jaxpr/all_gather | solution.py:113
  526.1 31.5 %all_gather.97 = bf16[768,192]{1,0:T(8,128)(2,1)S(1)} all-gather(bf16[96,192]{1,0:T(8,128)(2,1)} %get-tuple-element.1702), channel_id=1, replica_groups=mesh['dp'=8,'tensor'=4] {'dp'}, dimensions={0}, use_global_device_ids=true | all-gather | bytes 331776 | tf_op jit(solution)/shard_map/while/body/eval_jaxpr/all_gather | solution.py:108
  559.1 31.0 %all_gather.96 = bf16[768,192]{1,0:T(8,128)(2,1)S(1)} all-gather(bf16[96,192]{1,0:T(8,128)(2,1)S(1)} %copy-done.36), channel_id=1, replica_groups=mesh['dp'=8,'tensor'=4] {'dp'}, dimensions={0}, use_global_device_ids=true | all-gather | bytes 331776 | tf_op jit(solution)/shard_map/while/body/eval_jaxpr/all_gather | solution.py:106
  609.2 27.0 %reduce-scatter.28.cloned.1.call-done = bf16[256,768]{1,0:T(8,128)(2,1)} async-done(((bf16[1024,768]{1,0:T(8,128)(2,1)}), bf16[256,768]{1,0:T(8,128)(2,1)}) %reduce-scatter.28.cloned.1.call-update) | async-done | bytes 393232 | tf_op jit(solution)/shard_map/while/body/eval_jaxpr/reduce_scatter | solution.py:160
  676.3 39.1 %all-gather.20.cloned.1.call-done = bf16[768,768]{1,0:T(8,128)(2,1)} async-done(((bf16[96,768]{1,0:T(8,128)(2,1)}), bf16[768,768]{1,0:T(8,128)(2,1)}) %all-gather.20.cloned.1.call-update) | async-done | bytes 1179664 | tf_op jit(solution)/shard_map/while/body/eval_jaxpr/all_gather | solution.py:110
  721.8 36.0 %all-gather.22.cloned.1.call-done = bf16[768,768]{0,1:T(8,128)(2,1)} async-done(((bf16[768,96]{0,1:T(8,128)(2,1)}), bf16[768,768]{0,1:T(8,128)(2,1)}) %all-gather.22.cloned.1.call-update) | async-done | bytes 1179664 | tf_op jit(solution)/shard_map/while/body/eval_jaxpr/all_gather | solution.py:114
  825.8 28.3 %reduce-scatter.32.cloned.1.call-done = bf16[256,768]{1,0:T(8,128)(2,1)} async-done(((bf16[1024,768]{1,0:T(8,128)(2,1)}), bf16[256,768]{1,0:T(8,128)(2,1)}) %reduce-scatter.32.cloned.1.call-update) | async-done | bytes 393232 | tf_op jit(solution)/shard_map/while/body/eval_jaxpr/reduce_scatter | solution.py:195
  884.2 40.6 %while.97 = (s32[]{:T(128)}, f32[1024,3,64]{0,2,1:T(8,128)S(1)}, f32[1024,3,64]{0,2,1:T(8,128)}, f32[2,512,3,64]{1,0,3,2:T(2,128)}, bf16[2,512,3,64]{1,3,2,0:T(8...) while((s32[]{:T(128)}, f32[1024,3,64]{0,2,1:T(8,128)S(1)}, ...), condition=%wide.region_18.18_spmd.clone, body=%wide.region_16.17_spmd.clone.sunk | while | flops 1031830016 | bytes 56418472 | solution.py:248
  976.4 39.7 %all-reduce = (f32[768]{0:T(1024)}, f32[768]{0:T(1024)}, f32[768]{0:T(1024)}, f32[768]{0:T(1024)}) all-reduce(f32[768]{0:T(1024)S(1)} %copy-done.61, f32[768]{0:T(1024)S(1)} %copy-done.58, f32[768]{0:T(1024)S(1)} %copy-done.55, f32[768]{0:T(1024)S(1)} %copy-done.52), channel_id=1, replica_groups=mesh['dp'=8,'tensor'=4] {'dp','tensor'}, use_global_device_ids=true, to_apply=%region_32.33 | all-reduce | flops 3072 | bytes 24576 | tf_op jit(solution)/shard_map/psum | solution.py:321
  1033.9 64.2 %reduce-scatter.14.cloned.1.call-done = f32[96,192]{1,0:T(8,128)} async-done(((f32[768,192]{1,0:T(8,128)}), f32[96,192]{1,0:T(8,128)}) %reduce-scatter.14.cloned.1.call-update) | async-done | bytes 73744 | tf_op jit(solution)/shard_map/reduce_scatter | solution.py:316
  1098.1 65.5 %reduce-scatter.16.cloned.1.call-done = f32[96,192]{1,0:T(8,128)} async-done(((f32[768,192]{1,0:T(8,128)}), f32[96,192]{1,0:T(8,128)}) %reduce-scatter.16.cloned.1.call-update) | async-done | bytes 73744 | tf_op jit(solution)/shard_map/reduce_scatter | solution.py:316
  1163.6 65.9 %reduce-scatter.18.cloned.1.call-done = f32[96,192]{1,0:T(8,128)} async-done(((f32[768,192]{1,0:T(8,128)}), f32[96,192]{1,0:T(8,128)}) %reduce-scatter.18.cloned.1.call-update) | async-done | bytes 73744 | tf_op jit(solution)/shard_map/reduce_scatter | solution.py:316
  1229.5 72.1 %reduce-scatter.20.cloned.1.call-done = f32[96,768]{1,0:T(8,128)} async-done(((f32[768,768]{1,0:T(8,128)}), f32[96,768]{1,0:T(8,128)}) %reduce-scatter.20.cloned.1.call-update) | async-done | bytes 294928 | tf_op jit(solution)/shard_map/reduce_scatter | solution.py:316
  1301.6 72.1 %reduce-scatter.22.cloned.1.call-done = f32[96,768]{1,0:T(8,128)} async-done(((f32[768,768]{1,0:T(8,128)}), f32[96,768]{1,0:T(8,128)}) %reduce-scatter.22.cloned.1.call-update) | async-done | bytes 294928 | tf_op jit(solution)/shard_map/reduce_scatter | solution.py:316
  1373.7 72.0 %reduce-scatter.24.cloned.1.call-done = f32[768,96]{0,1:T(8,128)} async-done(((f32[768,768]{0,1:T(8,128)}), f32[768,96]{0,1:T(8,128)}) %reduce-scatter.24.cloned.1.call-update) | async-done | bytes 294928 | tf_op jit(solution)/shard_map/reduce_scatter | solution.py:319
  (613 shorter events, 553.5 us)
Async XLA Ops:
  14.8 101.6 %all-gather.14.cloned.1.call-start = ((), (), s32[]{:S(2)}) async-start(), calls=%async_computation.18 | async-start | bytes 1966080 | tf_op jit(solution)/shard_map/while/body/eval_jaxpr/all_gather | solution.py:120
  16.6 145.9 %reduce-scatter.28.cloned.1.call-start = ((), (), s32[]{:S(2)}) async-start(), calls=%async_computation.19 | async-start | bytes 1966080 | tf_op jit(solution)/shard_map/while/body/eval_jaxpr/reduce_scatter | solution.py:160
  17.7 65.9 %collective-permute-start = (bf16[2,96,192]{2,1,0:T(8,128)(2,1)S(1)}, bf16[2,96,192]{2,1,0:T(8,128)(2,1)S(1)}, u32[]{:S(2)}, u32[]{:S(2)}) collective-permute-start(bf16[2,96,192]{2,1,0:T(8,128)(2,1)S(1)} %get-tuple-element.1484), channel_id=1, source_target_pairs={{0,8},{4,12},{8,0},{12,4},{16,24},{20,28},{24,16},{28,20},{1,9},{5... | collective-permute-start | bytes 221192 | tf_op jit(solution)/shard_map/while/body/eval_jaxpr/ppermute | solution.py:23
  135.1 62.7 %all-gather.16.cloned.1.call-start = ((), (), s32[]{:S(2)}) async-start(), calls=%async_computation.20 | async-start | bytes 1966080 | tf_op jit(solution)/shard_map/while/body/eval_jaxpr/all_gather | solution.py:168
  167.0 74.7 %all-gather.20.cloned.1.call-start = ((), (), s32[]{:S(2)}) async-start(), calls=%async_computation.22 | async-start | bytes 1327104 | tf_op jit(solution)/shard_map/while/body/eval_jaxpr/all_gather | solution.py:110
  167.6 116.6 %all-gather.22.cloned.1.call-start = ((), (), s32[]{:S(2)}) async-start(), calls=%async_computation.23 | async-start | bytes 1327104 | tf_op jit(solution)/shard_map/while/body/eval_jaxpr/all_gather | solution.py:114
  168.3 147.0 %reduce-scatter.30.cloned.1.call-start = ((), (), s32[]{:S(2)}) async-start(), calls=%async_computation.24 | async-start | bytes 1966080 | tf_op jit(solution)/shard_map/while/body/eval_jaxpr/reduce_scatter | solution.py:175
  321.8 58.6 %reduce-scatter.32.cloned.1.call-start = ((), (), s32[]{:S(2)}) async-start(), calls=%async_computation.26 | async-start | bytes 1966080 | tf_op jit(solution)/shard_map/while/body/eval_jaxpr/reduce_scatter | solution.py:195
  386.7 101.0 %reduce-scatter.34.cloned.1.call-start = ((), (), s32[]{:S(2)}) async-start(), calls=%async_computation.28 | async-start | bytes 1966080 | tf_op jit(solution)/shard_map/while/body/eval_jaxpr/reduce_scatter | solution.py:267
  489.8 100.6 %all-gather.14.cloned.1.call-start = ((), (), s32[]{:S(2)}) async-start(), calls=%async_computation.18 | async-start | bytes 1966080 | tf_op jit(solution)/shard_map/while/body/eval_jaxpr/all_gather | solution.py:120
  491.7 144.5 %reduce-scatter.28.cloned.1.call-start = ((), (), s32[]{:S(2)}) async-start(), calls=%async_computation.19 | async-start | bytes 1966080 | tf_op jit(solution)/shard_map/while/body/eval_jaxpr/reduce_scatter | solution.py:160
  492.7 65.0 %collective-permute-start = (bf16[2,96,192]{2,1,0:T(8,128)(2,1)S(1)}, bf16[2,96,192]{2,1,0:T(8,128)(2,1)S(1)}, u32[]{:S(2)}, u32[]{:S(2)}) collective-permute-start(bf16[2,96,192]{2,1,0:T(8,128)(2,1)S(1)} %get-tuple-element.1484), channel_id=1, source_target_pairs={{0,8},{4,12},{8,0},{12,4},{16,24},{20,28},{24,16},{28,20},{1,9},{5... | collective-permute-start | bytes 221192 | tf_op jit(solution)/shard_map/while/body/eval_jaxpr/ppermute | solution.py:23
  609.1 62.4 %all-gather.16.cloned.1.call-start = ((), (), s32[]{:S(2)}) async-start(), calls=%async_computation.20 | async-start | bytes 1966080 | tf_op jit(solution)/shard_map/while/body/eval_jaxpr/all_gather | solution.py:168
  640.7 74.7 %all-gather.20.cloned.1.call-start = ((), (), s32[]{:S(2)}) async-start(), calls=%async_computation.22 | async-start | bytes 1327104 | tf_op jit(solution)/shard_map/while/body/eval_jaxpr/all_gather | solution.py:110
  641.3 116.6 %all-gather.22.cloned.1.call-start = ((), (), s32[]{:S(2)}) async-start(), calls=%async_computation.23 | async-start | bytes 1327104 | tf_op jit(solution)/shard_map/while/body/eval_jaxpr/all_gather | solution.py:114
  642.0 147.1 %reduce-scatter.30.cloned.1.call-start = ((), (), s32[]{:S(2)}) async-start(), calls=%async_computation.24 | async-start | bytes 1966080 | tf_op jit(solution)/shard_map/while/body/eval_jaxpr/reduce_scatter | solution.py:175
  860.4 100.7 %reduce-scatter.34.cloned.1.call-start = ((), (), s32[]{:S(2)}) async-start(), calls=%async_computation.28 | async-start | bytes 1966080 | tf_op jit(solution)/shard_map/while/body/eval_jaxpr/reduce_scatter | solution.py:267
  965.8 66.4 %reduce-scatter.26.cloned.1.call-start = ((), (), s32[]{:S(2)}) async-start(), calls=%async_computation.17 | async-start | bytes 884736
  968.3 129.9 %reduce-scatter.14.cloned.1.call-start = ((), (), s32[]{:S(2)}) async-start(), calls=%async_computation.11 | async-start | bytes 884736 | tf_op jit(solution)/shard_map/reduce_scatter | solution.py:316
  969.5 194.1 %reduce-scatter.16.cloned.1.call-start = ((), (), s32[]{:S(2)}) async-start(), calls=%async_computation.12 | async-start | bytes 884736 | tf_op jit(solution)/shard_map/reduce_scatter | solution.py:316
  970.8 258.7 %reduce-scatter.18.cloned.1.call-start = ((), (), s32[]{:S(2)}) async-start(), calls=%async_computation.13 | async-start | bytes 884736 | tf_op jit(solution)/shard_map/reduce_scatter | solution.py:316
  972.0 329.6 %reduce-scatter.20.cloned.1.call-start = ((), (), s32[]{:S(2)}) async-start(), calls=%async_computation.14 | async-start | bytes 2654208 | tf_op jit(solution)/shard_map/reduce_scatter | solution.py:316
  972.8 400.9 %reduce-scatter.22.cloned.1.call-start = ((), (), s32[]{:S(2)}) async-start(), calls=%async_computation.15 | async-start | bytes 2654208 | tf_op jit(solution)/shard_map/reduce_scatter | solution.py:316
  973.5 472.1 %reduce-scatter.24.cloned.1.call-start = ((), (), s32[]{:S(2)}) async-start(), calls=%async_computation.16 | async-start | bytes 2654208 | tf_op jit(solution)/shard_map/reduce_scatter | solution.py:319
  (152 other events, 2036.2 us)
Sparse Core Ops, SparseCore 0:
  17.2 21.3 all-gather.13
  134.7 27.7 reduce-scatter.27
  288.7 26.6 reduce-scatter.29
  352.2 28.1 reduce-scatter.31
  459.4 28.1 reduce-scatter.33
  491.9 19.6 all-gather.13
  608.6 27.4 reduce-scatter.27
  762.4 26.6 reduce-scatter.29
  825.9 28.1 reduce-scatter.31
  932.9 28.2 reduce-scatter.33
Sparse Core Ops, SparseCore 1:
  137.2 41.1 all-gather.17
  179.8 18.0 all-gather.15
  200.2 41.5 all-gather.19
  244.2 40.0 all-gather.21
  321.9 19.5 all-gather.23
  386.8 19.5 all-gather.25
  611.2 40.8 all-gather.17
  653.6 17.9 all-gather.15
  673.8 41.5 all-gather.19
  717.8 40.0 all-gather.21
  795.6 19.5 all-gather.23
  860.5 19.5 all-gather.25
  969.6 62.6 reduce-scatter.25
  1036.5 61.5 reduce-scatter.13
  1102.0 61.5 reduce-scatter.15
  1167.9 61.5 reduce-scatter.17
  1233.6 68.0 reduce-scatter.19
  1305.7 68.0 reduce-scatter.21
  1377.6 68.0 reduce-scatter.23
